TPU v7x, 32 devices: a whole 2x2x4 slice. The times are simulated.
32 devices in a mesh: dom: 2 (over y), row: 4 (over z), nbr: 4 (over x, core).
Axes of the slice: x: 2, y: 2, z: 4, core: 2. Of those that a mesh axis runs over, the one named last changes fastest.
Arguments:
- blocks: float32 [24, 12, 128, 128], P(('dom', 'row'), 'nbr'), parts along dimension 0, may hold values from -0.15625 to 0.15625
- partner_ids: int32 [24, 12], P(('dom', 'row'), 'nbr'), parts along dimension 0, may hold values from 0 to 11, as said below
- counts: int32 [24], P(('dom', 'row')), parts along dimension 0, may hold values from 1 to 12, as said below
- start: float32 [3072, 32], P(('dom', 'row')), parts along dimension 0, may hold values from -6 to 6
Outputs:
- basis: float32 [3072, 32], P(('dom', 'row')), parts along dimension 0
- ritz: float32 [64, 32], P('dom'), parts along dimension 0
There are 2 independent parts, one for each index of `dom`. A program takes and returns all parts, laid end to end along the dimension named above; each array names one. Nothing has to cross between parts.
Inputs may be any that keep to these rules, and one draw needn't show every extreme that they name: partner_ids[i,0] == i; slots 1 to counts[i] - 1 hold distinct block columns greater than i; slots from counts[i] on hold i. counts[i] <= min(12, 12 - i); counts[0] == 12.
All inputs are finite; a program needn't handle non-finite values.
Results may differ from a plain program's by a relative error of at most 0.0001.
Values sent between devices are 32-bit elements; how exact they have to be, the bound alone decides.
A program may use at most 64 MiB of HBM per device.

v0:
```python
import jax
import jax.numpy as jnp
from jax import lax
from jax.sharding import PartitionSpec as P

ITERS = 2
HIGH = lax.Precision.HIGHEST


def orthonormal(image, gram, total):
    lower = jnp.linalg.cholesky(gram / total)
    return lax.linalg.triangular_solve(lower, image, left_side=False, lower=True, transpose_a=True)


def body(blocks, partner_ids, counts, start):
    block_rows, slots_here = partner_ids.shape
    block_size = blocks.shape[2]
    columns = start.shape[1]
    row_count = lax.axis_size("row")
    all_blocks = block_rows * row_count
    total = all_blocks * block_size
    first_row = lax.axis_index("row") * block_rows
    rows_here = first_row + jnp.arange(block_rows, dtype=jnp.int32)
    slot_index = lax.axis_index("nbr") * slots_here + jnp.arange(slots_here, dtype=jnp.int32)
    valid = slot_index[None, :] < counts[:, None]
    weight = jnp.where(valid, jnp.where(partner_ids == rows_here[:, None], 0.5, 1.0), 0.0).astype(
        jnp.float32
    )
    targets = jnp.concatenate([partner_ids.reshape(-1), rows_here])
    whole = lax.all_gather(start, "row", axis=0, tiled=True)
    cross = jnp.zeros((columns, columns), jnp.float32)
    prior = start
    for step in range(ITERS):
        tiles = whole.reshape(all_blocks, block_size, columns)
        far = tiles[partner_ids] * weight[:, :, None, None]
        near = lax.dynamic_slice_in_dim(tiles, first_row, block_rows, 0)
        direct = jnp.einsum("ipab,ipbk->iak", blocks, far, precision=HIGH)
        transposed = (
            jnp.einsum("ipab,iak->ipbk", blocks, near, precision=HIGH) * weight[:, :, None, None]
        )
        items = jnp.concatenate(
            [transposed.reshape(block_rows * slots_here, block_size, columns), direct], axis=0
        )
        placed = jnp.zeros((all_blocks, block_size, columns), jnp.float32).at[targets].add(items)
        summed = lax.psum_scatter(
            placed.reshape(total, columns), "row", scatter_dimension=0, tiled=True
        )
        image = lax.psum(summed, "nbr")
        gram, cross = lax.psum(
            (jnp.dot(image.T, image, precision=HIGH), jnp.dot(prior.T, image, precision=HIGH)),
            "row",
        )
        cross = cross / total
        prior = orthonormal(image, gram, total)
        if step + 1 < ITERS:
            whole = lax.all_gather(prior, "row", axis=0, tiled=True)
    return (prior, cross)


def solution(mesh):
    return jax.shard_map(
        body,
        mesh=mesh,
        in_specs=(
            P(("dom", "row"), "nbr", None, None),
            P(("dom", "row"), "nbr"),
            P(("dom", "row")),
            P(("dom", "row"), None),
        ),
        out_specs=(P(("dom", "row"), None), P("dom", None)),
        check_vma=False,
    )
```

profile of v0, /device:TPU:0, one launch (start us, length us, event | category | flops | bytes accessed | tf_op | source)
XLA Modules:
  0.0 162.5 jit_solution(3839742283190382437)
XLA Ops:
  7.2 0.0 copy-start
  7.2 0.0 copy-start.1
  7.2 0.0 reduce-scatter.3.cloned.1.call-start
  7.2 0.8 concatenate.32
  8.1 0.0 copy-done.1
  8.1 0.1 reshape.123
  8.2 15.7 %all_gather.6 = f32[1536,32]{0,1:T(8,128)S(1)} all-gather(f32[384,32]{0,1:T(8,128)} %param.10), channel_id=1, replica_groups=mesh['dom'=2,'row'=4,'nbr'=4] {'row'}, dimensions={0}, use_global_device_ids=true | all-gather | bytes 245760 | tf_op jit(solution)/shard_map/all_gather | solution.py:30
  23.9 0.6 gather_fusion
  24.4 0.0 copy-start.2
  24.4 0.6 copy-done.2
  25.1 0.1 select_select_fusion.2
  25.2 0.0 copy-done
  25.2 0.5 convolution_multiply_fusion.1
  25.6 0.8 convolution_bitcast_fusion.3
  26.4 0.1 fusion.16
  26.5 1.1 scatter_fusion
  27.6 0.7 copy_bitcast_fusion.1
  28.3 0.0 reduce-scatter.3.cloned.1.call-update
  28.3 0.0 reduce-scatter.5.cloned.1.call-start
  28.4 21.0 %reduce-scatter.3.cloned.1.call-done = f32[384,32]{0,1:T(8,128)} async-done(((f32[1536,32]{0,1:T(8,128)}), f32[384,32]{0,1:T(8,128)}) %reduce-scatter.3.cloned.1.call-update) | async-done | bytes 49168 | tf_op jit(solution)/shard_map/reduce_scatter | solution.py:45
  49.4 11.0 %psum.35 = f32[384,32]{0,1:T(8,128)S(1)} all-reduce(f32[384,32]{0,1:T(8,128)} %reduce-scatter.3.cloned.1.call-done), channel_id=1, replica_groups=mesh['dom'=2,'row'=4,'nbr'=4] {'nbr'}, use_global_device_ids=true, to_apply=%region_2.3 | all-reduce | flops 12288 | bytes 98304 | tf_op jit(solution)/shard_map/psum | solution.py:48
  60.4 0.2 fusion.20
  60.6 15.9 %psum.36 = f32[32,32]{0,1:T(8,128)S(1)} all-reduce(f32[32,32]{0,1:T(8,128)S(1)} %fusion.20), channel_id=1, replica_groups=mesh['dom'=2,'row'=4,'nbr'=4] {'row'}, use_global_device_ids=true, to_apply=%region_3.4 | all-reduce | flops 1024 | bytes 8192 | tf_op jit(solution)/shard_map/psum | solution.py:49
  76.5 0.1 copy.30
  76.6 2.9 %cholesky.44 = f32[32,32]{1,0:T(8,128)S(1)} custom-call(f32[32,32]{1,0:T(8,128)S(1)} %fusion.13), custom_call_target="Cholesky" | custom-call | tf_op jit(solution)/shard_map/jit(cholesky)/cholesky | solution.py:11
  79.5 0.6 compare_reduce_fusion.1
  80.2 0.7 fusion.8
  80.8 2.4 %custom-call.6 = f32[1,32,32]{1,2,0:T(8,128)S(1)} custom-call(f32[1,32,32]{2,1,0:T(8,128)S(1)} %fusion.8), custom_call_target="InvertDiagBlocksLowerTriangular" | custom-call | tf_op jit(solution)/shard_map/triangular_solve/custom-call.0 | solution.py:12
  83.3 0.3 convolution_bitcast_fusion.2
  83.5 13.6 %all_gather.7 = f32[1536,32]{0,1:T(8,128)S(1)} all-gather(f32[384,32]{0,1:T(8,128)S(1)} %convolution_bitcast_fusion.2), channel_id=1, replica_groups=mesh['dom'=2,'row'=4,'nbr'=4] {'row'}, dimensions={0}, use_global_device_ids=true | all-gather | bytes 245760 | tf_op jit(solution)/shard_map/all_gather | solution.py:56
  97.1 0.6 gather_fusion.1
  97.7 0.5 convolution_multiply_fusion
  98.2 0.8 convolution_bitcast_fusion.1
  99.0 1.1 scatter_fusion.1
  100.1 0.7 copy_bitcast_fusion
  100.8 0.0 reduce-scatter.5.cloned.1.call-update
  100.8 18.8 %reduce-scatter.5.cloned.1.call-done = f32[384,32]{0,1:T(8,128)} async-done(((f32[1536,32]{0,1:T(8,128)}), f32[384,32]{0,1:T(8,128)}) %reduce-scatter.5.cloned.1.call-update) | async-done | bytes 49168 | tf_op jit(solution)/shard_map/reduce_scatter | solution.py:45
  119.6 11.0 %psum.37 = f32[384,32]{0,1:T(8,128)S(1)} all-reduce(f32[384,32]{0,1:T(8,128)} %reduce-scatter.5.cloned.1.call-done), channel_id=1, replica_groups=mesh['dom'=2,'row'=4,'nbr'=4] {'nbr'}, use_global_device_ids=true, to_apply=%region_8.11 | all-reduce | flops 12288 | bytes 98304 | tf_op jit(solution)/shard_map/psum | solution.py:48
  130.6 0.2 fusion.22
  130.8 0.2 fusion.21
  131.0 16.2 %all-reduce = (f32[32,32]{0,1:T(8,128)S(1)}, f32[32,32]{0,1:T(8,128)S(1)}) all-reduce(f32[32,32]{0,1:T(8,128)S(1)} %fusion.21, f32[32,32]{0,1:T(8,128)S(1)} %fusion.22), channel_id=1, replica_groups=mesh['dom'=2,'row'=4,'nbr'=4] {'row'}, use_global_device_ids=true, to_apply=%region_9.12 | all-reduce | flops 2048 | bytes 16384 | tf_op jit(solution)/shard_map/psum | solution.py:49
  147.3 0.7 copy.37
  148.0 0.1 copy.35
  148.0 2.9 %cholesky.55 = f32[32,32]{1,0:T(8,128)S(1)} custom-call(f32[32,32]{1,0:T(8,128)S(1)} %fusion.11), custom_call_target="Cholesky" | custom-call | tf_op jit(solution)/shard_map/jit(cholesky)/cholesky | solution.py:11
  151.0 0.6 compare_reduce_fusion
  151.6 0.7 fusion.9
  152.3 2.4 %custom-call.7 = f32[1,32,32]{1,2,0:T(8,128)S(1)} custom-call(f32[1,32,32]{2,1,0:T(8,128)S(1)} %fusion.9), custom_call_target="InvertDiagBlocksLowerTriangular" | custom-call | tf_op jit(solution)/shard_map/triangular_solve/custom-call.0 | solution.py:12
  154.7 0.9 convolution_bitcast_fusion
  (17 shorter events, 0.2 us)
Async XLA Ops:
  7.2 18.0 %copy-start = (f32[3,3,128,128]{3,2,1,0:T(8,128)S(1)}, f32[3,3,128,128]{3,2,1,0:T(8,128)}, u32[]{:S(2)}) copy-start(f32[3,3,128,128]{3,2,1,0:T(8,128)} %param.7) | copy-start | bytes 1769476
  7.2 0.9 copy-start.1
  7.2 42.2 %reduce-scatter.3.cloned.1.call-start = ((), (), s32[]{:S(2)}) async-start(), calls=%async_computation.2 | async-start | bytes 245760 | tf_op jit(solution)/shard_map/reduce_scatter | solution.py:45
  24.4 0.7 copy-start.2
  28.3 91.3 %reduce-scatter.5.cloned.1.call-start = ((), (), s32[]{:S(2)}) async-start(), calls=%async_computation.3 | async-start | bytes 245760 | tf_op jit(solution)/shard_map/reduce_scatter | solution.py:45
Sparse Core Ops, SparseCore 0:
  28.4 20.9 reduce-scatter.2
  100.9 18.6 reduce-scatter.4
where the time goes:
time: 163 us; the launch traced here: 162 us
  blocking collectives  83.4 us (51%)
  waiting for transfers between devices  39.9 us (24%)
  other arithmetic  15.8 us (10%)
  between operations  14.3 us (9%)
  local copies, waits for them, and re-layouts  4.93 us (3%)
  matrix products  4.18 us (3%)
    reduce_scatter x2, waiting for transfers between devices, body(): lax.psum_scatter(placed.reshape(total, columns), 'row', scatter_dimension...  39.8 us
    psum x2, blocking collectives, body(): lax.psum((jnp.dot(image.T, image, precision=HIGH), jnp.dot(prior.T, image...  32.1 us
    psum x2, blocking collectives, body(): image = lax.psum(summed, 'nbr')  22 us
    all_gather x1, blocking collectives, body(): whole = lax.all_gather(start, 'row', axis=0, tiled=True)  15.7 us
    all_gather x1, blocking collectives, body(): whole = lax.all_gather(prior, 'row', axis=0, tiled=True)  13.6 us
    another operation x6, other arithmetic, orthonormal(): lower = jnp.linalg.cholesky(gram / total)  7.19 us
    another operation x4, other arithmetic, orthonormal(): lax.linalg.triangular_solve(lower, image, left_side=False, lower=True, tr...  6.17 us
  transfers between devices with their start and end apart: 2, of which 2 were waited for; matrix products, arithmetic and copies ran while one was open for 0% of the time, Pallas kernels for 0%

commit v1 on v0

--- a/solution.py
+++ b/solution.py
@@ -27,7 +27,12 @@
         jnp.float32
     )
     targets = jnp.concatenate([partner_ids.reshape(-1), rows_here])
-    whole = lax.all_gather(start, "row", axis=0, tiled=True)
+    ring = [start]
+    for hop in range(3):
+        ring.append(lax.ppermute(ring[-1], "row", [(dev, (dev + 1) % 4) for dev in range(4)]))
+    whole = jnp.roll(
+        jnp.concatenate(ring[::-1], axis=0), (lax.axis_index("row") + 1) * ring[0].shape[0], axis=0
+    )
     cross = jnp.zeros((columns, columns), jnp.float32)
     prior = start
     for step in range(ITERS):

time: 163 us -> 163 us (level)
  blocking collectives: 83.4 us -> 67.6 us
  waiting for transfers between devices: 39.9 us -> 51.4 us
  starting transfers between devices: 0.08 us -> 3.19 us
    all_gather x1 -> x0, blocking collectives: 15.7 us -> none  [body(): whole = lax.all_gather(start, 'row', axis=0, tiled=True)]
    ppermute x0 -> x3, waiting for transfers between devices: none -> 14.4 us  [body(): lax.ppermute(ring[-1], 'row', [(dev, (dev + 1) % 4) for dev in range(4)])]
    ppermute x0 -> x3, starting transfers between devices: none -> 3.11 us  [body(): lax.ppermute(ring[-1], 'row', [(dev, (dev + 1) % 4) for dev in range(4)])]
    reduce_scatter x2, waiting for transfers between devices: 39.8 us -> 36.9 us  [body(): lax.psum_scatter(placed.reshape(total, columns), 'row', scatter_dimension...]
  transfers between devices with their start and end apart: 2 -> 5, of which waited for: 2 -> 5; matrix products, arithmetic and copies ran while one was open for 0% -> 0% of each run, Pallas kernels for 0% -> 0%
where the time goes in v1:
time: 163 us; the launch traced here: 162 us
  blocking collectives  67.6 us (41%)
  waiting for transfers between devices  51.4 us (32%)
  other arithmetic  15.8 us (10%)
  between operations  14.3 us (9%)
  local copies, waits for them, and re-layouts  5.81 us (4%)
  matrix products  4.2 us (3%)
  starting transfers between devices  3.19 us (2%)
    reduce_scatter x2, waiting for transfers between devices, body(): lax.psum_scatter(placed.reshape(total, columns), 'row', scatter_dimension...  36.9 us
    psum x2, blocking collectives, body(): lax.psum((jnp.dot(image.T, image, precision=HIGH), jnp.dot(prior.T, image...  32 us
    psum x2, blocking collectives, body(): image = lax.psum(summed, 'nbr')  22 us
    ppermute x3, waiting for transfers between devices, body(): lax.ppermute(ring[-1], 'row', [(dev, (dev + 1) % 4) for dev in range(4)])  14.4 us
    all_gather x1, blocking collectives, body(): whole = lax.all_gather(prior, 'row', axis=0, tiled=True)  13.6 us
    another operation x6, other arithmetic, orthonormal(): lower = jnp.linalg.cholesky(gram / total)  7.19 us
    another operation x4, other arithmetic, orthonormal(): lax.linalg.triangular_solve(lower, image, left_side=False, lower=True, tr...  6.17 us
  transfers between devices with their start and end apart: 5, of which 5 were waited for; matrix products, arithmetic and copies ran while one was open for 0% of the time, Pallas kernels for 0%

profile of v1, /device:TPU:0, one launch (start us, length us, event | category | flops | bytes accessed | tf_op | source)
XLA Modules:
  0.0 162.2 jit_solution(13400582840526321598)
XLA Ops:
  7.2 0.0 reduce-scatter.3.cloned.1.call-start
  7.2 3.1 %collective-permute-start = (f32[384,32]{0,1:T(8,128)}, f32[384,32]{0,1:T(8,128)S(1)}, u32[]{:S(2)}, u32[]{:S(2)}) collective-permute-start(f32[384,32]{0,1:T(8,128)} %param.10), channel_id=1, source_target_pairs={{0,4},{4,8},{8,12},{12,0},{1,5},{5,9},{9,13},{13,1},{2,6},{6,10},{... | collective-permute-start | bytes 147464 | tf_op jit(solution)/shard_map/ppermute | solution.py:32
  10.3 0.7 copy-done.2
  11.0 0.1 reshape.123
  11.1 0.7 copy-done.3
  11.8 0.1 select_select_fusion.2
  11.8 2.8 %collective-permute-done = f32[384,32]{0,1:T(8,128)S(1)} collective-permute-done((f32[384,32]{0,1:T(8,128)}, f32[384,32]{0,1:T(8,128)S(1)}, u32[]{:S(2)}, u32[]{:S(2)}) %collective-permute-start) | collective-permute-done | bytes 49184 | tf_op jit(solution)/shard_map/ppermute | solution.py:32
  14.6 0.1 concatenate.38
  14.7 5.8 %collective-permute-done.1 = f32[384,32]{0,1:T(8,128)S(1)} collective-permute-done((f32[384,32]{0,1:T(8,128)S(1)}, f32[384,32]{0,1:T(8,128)S(1)}, u32[]{:S(2)}, u32[]{:S(2)}) %collective-permute-start.1) | collective-permute-done | bytes 49184 | tf_op jit(solution)/shard_map/ppermute | solution.py:32
  20.5 0.1 fusion.18
  20.6 5.8 %collective-permute-done.2 = f32[384,32]{0,1:T(8,128)S(1)} collective-permute-done((f32[384,32]{0,1:T(8,128)S(1)}, f32[384,32]{0,1:T(8,128)S(1)}, u32[]{:S(2)}, u32[]{:S(2)}) %collective-permute-start.2) | collective-permute-done | bytes 49184 | tf_op jit(solution)/shard_map/ppermute | solution.py:32
  26.5 0.8 copy-done.1
  27.3 0.1 copy_bitcast_fusion.3
  27.4 0.6 gather_fusion
  28.0 0.5 convolution_multiply_fusion.1
  28.5 0.8 convolution_bitcast_fusion.3
  29.3 1.1 scatter_fusion
  30.4 0.7 copy_bitcast_fusion.1
  31.1 0.0 reduce-scatter.3.cloned.1.call-update
  31.1 0.0 reduce-scatter.5.cloned.1.call-start
  31.1 18.1 %reduce-scatter.3.cloned.1.call-done = f32[384,32]{0,1:T(8,128)} async-done(((f32[1536,32]{0,1:T(8,128)}), f32[384,32]{0,1:T(8,128)}) %reduce-scatter.3.cloned.1.call-update) | async-done | bytes 49168 | tf_op jit(solution)/shard_map/reduce_scatter | solution.py:50
  49.3 11.0 %psum.35 = f32[384,32]{0,1:T(8,128)S(1)} all-reduce(f32[384,32]{0,1:T(8,128)} %reduce-scatter.3.cloned.1.call-done), channel_id=1, replica_groups=mesh['dom'=2,'row'=4,'nbr'=4] {'nbr'}, use_global_device_ids=true, to_apply=%region_2.3 | all-reduce | flops 12288 | bytes 98304 | tf_op jit(solution)/shard_map/psum | solution.py:53
  60.3 0.2 fusion.20
  60.5 15.8 %psum.36 = f32[32,32]{0,1:T(8,128)S(1)} all-reduce(f32[32,32]{0,1:T(8,128)S(1)} %fusion.20), channel_id=1, replica_groups=mesh['dom'=2,'row'=4,'nbr'=4] {'row'}, use_global_device_ids=true, to_apply=%region_3.4 | all-reduce | flops 1024 | bytes 8192 | tf_op jit(solution)/shard_map/psum | solution.py:54
  76.3 0.1 copy.30
  76.4 2.9 %cholesky.44 = f32[32,32]{1,0:T(8,128)S(1)} custom-call(f32[32,32]{1,0:T(8,128)S(1)} %fusion.13), custom_call_target="Cholesky" | custom-call | tf_op jit(solution)/shard_map/jit(cholesky)/cholesky | solution.py:11
  79.4 0.6 compare_reduce_fusion.1
  80.0 0.7 fusion.8
  80.7 2.4 %custom-call.6 = f32[1,32,32]{1,2,0:T(8,128)S(1)} custom-call(f32[1,32,32]{2,1,0:T(8,128)S(1)} %fusion.8), custom_call_target="InvertDiagBlocksLowerTriangular" | custom-call | tf_op jit(solution)/shard_map/triangular_solve/custom-call.0 | solution.py:12
  83.1 0.3 convolution_bitcast_fusion.2
  83.4 13.6 %all_gather.3 = f32[1536,32]{0,1:T(8,128)S(1)} all-gather(f32[384,32]{0,1:T(8,128)S(1)} %convolution_bitcast_fusion.2), channel_id=1, replica_groups=mesh['dom'=2,'row'=4,'nbr'=4] {'row'}, dimensions={0}, use_global_device_ids=true | all-gather | bytes 245760 | tf_op jit(solution)/shard_map/all_gather | solution.py:61
  97.0 0.6 gather_fusion.1
  97.5 0.5 convolution_multiply_fusion
  98.0 0.8 convolution_bitcast_fusion.1
  98.8 1.1 scatter_fusion.1
  99.9 0.7 copy_bitcast_fusion
  100.6 18.8 %reduce-scatter.5.cloned.1.call-done = f32[384,32]{0,1:T(8,128)} async-done(((f32[1536,32]{0,1:T(8,128)}), f32[384,32]{0,1:T(8,128)}) %reduce-scatter.5.cloned.1.call-update) | async-done | bytes 49168 | tf_op jit(solution)/shard_map/reduce_scatter | solution.py:50
  119.4 11.0 %psum.37 = f32[384,32]{0,1:T(8,128)S(1)} all-reduce(f32[384,32]{0,1:T(8,128)} %reduce-scatter.5.cloned.1.call-done), channel_id=1, replica_groups=mesh['dom'=2,'row'=4,'nbr'=4] {'nbr'}, use_global_device_ids=true, to_apply=%region_8.11 | all-reduce | flops 12288 | bytes 98304 | tf_op jit(solution)/shard_map/psum | solution.py:53
  130.5 0.2 fusion.22
  130.6 0.2 fusion.21
  130.8 16.2 %all-reduce = (f32[32,32]{0,1:T(8,128)S(1)}, f32[32,32]{0,1:T(8,128)S(1)}) all-reduce(f32[32,32]{0,1:T(8,128)S(1)} %fusion.21, f32[32,32]{0,1:T(8,128)S(1)} %fusion.22), channel_id=1, replica_groups=mesh['dom'=2,'row'=4,'nbr'=4] {'row'}, use_global_device_ids=true, to_apply=%region_9.12 | all-reduce | flops 2048 | bytes 16384 | tf_op jit(solution)/shard_map/psum | solution.py:54
  147.0 0.1 copy.35
  147.1 2.9 %cholesky.55 = f32[32,32]{1,0:T(8,128)S(1)} custom-call(f32[32,32]{1,0:T(8,128)S(1)} %fusion.11), custom_call_target="Cholesky" | custom-call | tf_op jit(solution)/shard_map/jit(cholesky)/cholesky | solution.py:11
  150.1 0.6 compare_reduce_fusion
  150.7 0.7 fusion.9
  151.4 2.4 %custom-call.7 = f32[1,32,32]{1,2,0:T(8,128)S(1)} custom-call(f32[1,32,32]{2,1,0:T(8,128)S(1)} %fusion.9), custom_call_target="InvertDiagBlocksLowerTriangular" | custom-call | tf_op jit(solution)/shard_map/triangular_solve/custom-call.0 | solution.py:12
  153.8 0.9 convolution_bitcast_fusion
  154.7 0.7 copy.37
  (32 shorter events, 0.3 us)
Async XLA Ops:
  7.2 20.8 %copy-start = (f32[3,3,128,128]{3,2,1,0:T(8,128)S(1)}, f32[3,3,128,128]{3,2,1,0:T(8,128)}, u32[]{:S(2)}) copy-start(f32[3,3,128,128]{3,2,1,0:T(8,128)} %param.7) | copy-start | bytes 1769476
  7.2 42.1 %reduce-scatter.3.cloned.1.call-start = ((), (), s32[]{:S(2)}) async-start(), calls=%async_computation.2 | async-start | bytes 245760 | tf_op jit(solution)/shard_map/reduce_scatter | solution.py:50
  7.2 7.4 %collective-permute-start = (f32[384,32]{0,1:T(8,128)}, f32[384,32]{0,1:T(8,128)S(1)}, u32[]{:S(2)}, u32[]{:S(2)}) collective-permute-start(f32[384,32]{0,1:T(8,128)} %param.10), channel_id=1, source_target_pairs={{0,4},{4,8},{8,12},{12,0},{1,5},{5,9},{9,13},{13,1},{2,6},{6,10},{... | collective-permute-start | bytes 147464 | tf_op jit(solution)/shard_map/ppermute | solution.py:32
  10.3 0.7 copy-start.2
  11.1 0.7 copy-start.3
  14.6 5.9 %collective-permute-start.1 = (f32[384,32]{0,1:T(8,128)S(1)}, f32[384,32]{0,1:T(8,128)S(1)}, u32[]{:S(2)}, u32[]{:S(2)}) collective-permute-start(f32[384,32]{0,1:T(8,128)S(1)} %collective-permute-done), channel_id=1, source_target_pairs={{0,4},{4,8},{8,12},{12,0},{1,5},{5,9},{9,13},{13,1},{2,6},{6,10},{... | collective-permute-start | bytes 147464 | tf_op jit(solution)/shard_map/ppermute | solution.py:32
  20.5 5.9 %collective-permute-start.2 = (f32[384,32]{0,1:T(8,128)S(1)}, f32[384,32]{0,1:T(8,128)S(1)}, u32[]{:S(2)}, u32[]{:S(2)}) collective-permute-start(f32[384,32]{0,1:T(8,128)S(1)} %collective-permute-done.1), channel_id=1, source_target_pairs={{0,4},{4,8},{8,12},{12,0},{1,5},{5,9},{9,13},{13,1},{2,6},{6,10},{... | collective-permute-start | bytes 147464 | tf_op jit(solution)/shard_map/ppermute | solution.py:32
  26.4 0.8 copy-start.1
  31.1 88.3 %reduce-scatter.5.cloned.1.call-start = ((), (), s32[]{:S(2)}) async-start(), calls=%async_computation.3 | async-start | bytes 245760 | tf_op jit(solution)/shard_map/reduce_scatter | solution.py:50
Sparse Core Ops, SparseCore 0:
  31.2 18.0 reduce-scatter.2
  100.7 18.6 reduce-scatter.4
